TPU v7x, 32 devices: a whole 2x2x4 slice. The times are simulated.
32 devices in a mesh: blk: 2 (over core), head: 16 (over z, y, x).
Axes of the slice: x: 2, y: 2, z: 4, core: 2. Of those that a mesh axis runs over, the one named last changes fastest.
Arguments:
- tokens_qkv: bfloat16 [2048, 12288], P(('blk', 'head')), may hold values from -8 to 8, as said below
- block_mask: int32 [16, 16], replicated, may hold values from 0 to 1, as said below
Outputs:
- attended: bfloat16 [2048, 4096], P(('blk', 'head'))
Inputs may be any that keep to these rules, and one draw needn't show every extreme that they name: `tokens_qkv`: queries, keys and values ordered by head, then query, key, value, then the 128 entries. `block_mask`: 1 where a pair of 128-token blocks attends; a block always attends to itself whatever the entry says.
All inputs are finite; a program needn't handle non-finite values.
Results may differ from a plain program's by a relative error of at most 0.007.
Values may be sent and summed in bfloat16 or wider, within the bound.
No kernel may reach another device: no remote copies, remote signals or barrier semaphores. Data moves between devices by JAX's collectives and lax.ppermute only.
A program may use at most 64 MiB of HBM per device.

v0:
```python
import jax
import jax.numpy as jnp
from jax import lax
from jax.sharding import PartitionSpec as P

HD = 128
BLOCK = 128
NEGATIVE = -1e30


def shortened(x):

    def short(part):
        return part.astype(jnp.bfloat16) if part.dtype == jnp.float32 else part

    return jax.tree.map(short, x)


def shifted(x, axis, by):
    size = lax.axis_size(axis)
    return lax.ppermute(x, axis, [(i, (i + by) % size) for i in range(size)])


def live_pairs(block_mask, row_start, row_count, col_start, col_count):
    picked = lax.dynamic_slice(
        block_mask,
        (row_start // BLOCK, col_start // BLOCK),
        (row_count // BLOCK, col_count // BLOCK),
    )
    spread = jnp.broadcast_to(
        (picked == 1)[:, None, :, None], (row_count // BLOCK, BLOCK, col_count // BLOCK, BLOCK)
    ).reshape(row_count, col_count)
    row_blocks = (row_start + jnp.arange(row_count, dtype=jnp.int32)) // BLOCK
    col_blocks = (col_start + jnp.arange(col_count, dtype=jnp.int32)) // BLOCK
    return spread | (row_blocks[:, None] == col_blocks[None, :])


def attend(running, queries, keys_part, values_part, live_map):
    outputs, maxima, totals = running
    key_count = keys_part.shape[0]
    stride = min(key_count, 512)
    factor_scale = queries.shape[-1] ** (-0.5)
    for offset in range(0, key_count, stride):
        scores = (
            jnp.einsum(
                "qhd,khd->qhk",
                queries,
                keys_part[offset : offset + stride],
                preferred_element_type=jnp.float32,
            )
            * factor_scale
        )
        allowed = live_map[:, None, offset : offset + stride]
        scores = jnp.where(allowed, scores, NEGATIVE)
        newest = jnp.maximum(maxima, jnp.max(scores, axis=-1))
        weights = jnp.where(allowed, jnp.exp(scores - newest[..., None]), 0.0)
        factor = jnp.exp(maxima - newest)
        totals = totals * factor + jnp.sum(weights, axis=-1)
        outputs = outputs * factor[..., None] + jnp.einsum(
            "qhk,khd->qhd",
            weights.astype(jnp.bfloat16),
            values_part[offset : offset + stride],
            preferred_element_type=jnp.float32,
        )
        maxima = newest
    return (outputs, maxima, totals)


def empty_state(row_total, head_count):
    return (
        jnp.zeros((row_total, head_count, HD), jnp.float32),
        jnp.full((row_total, head_count), NEGATIVE, jnp.float32),
        jnp.zeros((row_total, head_count), jnp.float32),
    )


def on_device(tokens_qkv, block_mask):
    by_heads = lax.all_to_all(tokens_qkv, "head", split_axis=1, concat_axis=0, tiled=True)
    rows_here = by_heads.shape[0]
    head_count = by_heads.shape[1] // (3 * HD)
    packed = by_heads.reshape(rows_here, head_count, 3, HD)
    queries = packed[:, :, 0]
    keys_here = packed[:, :, 1]
    values_here = packed[:, :, 2]
    cycle_size = lax.axis_size("blk")
    own_index = lax.axis_index("blk")
    half_rows = rows_here // 2
    own_start = own_index * rows_here
    running = attend(
        empty_state(rows_here, head_count),
        queries,
        keys_here,
        values_here,
        live_pairs(block_mask, own_start, rows_here, own_start, rows_here),
    )

    def advance(hop_index, cycle_state):
        upward = shifted(shortened(cycle_state[1]), "blk", 1)
        downward = shifted(shortened(cycle_state[2]), "blk", -1)
        forward = (own_index - hop_index) % cycle_size
        backward = (own_index + hop_index) % cycle_size
        updated = attend(
            cycle_state[0],
            queries,
            upward[0],
            upward[1],
            live_pairs(block_mask, own_start, rows_here, forward * rows_here, half_rows),
        )
        updated = attend(
            updated,
            queries,
            downward[0],
            downward[1],
            live_pairs(
                block_mask, own_start, rows_here, backward * rows_here + half_rows, half_rows
            ),
        )
        return (updated, upward, downward)

    start_up = (keys_here[:half_rows], values_here[:half_rows])
    start_down = (keys_here[half_rows:], values_here[half_rows:])
    running, unused_up, unused_down = lax.fori_loop(
        1, cycle_size, advance, (running, start_up, start_down)
    )
    outputs, totals = (running[0], running[2])
    result = (outputs / totals[..., None]).astype(jnp.bfloat16).reshape(rows_here, head_count * HD)
    return lax.all_to_all(result, "head", split_axis=0, concat_axis=1, tiled=True)


def solution(mesh):
    return jax.shard_map(
        on_device,
        mesh=mesh,
        in_specs=(P(("blk", "head"), None), P()),
        out_specs=P(("blk", "head"), None),
        check_vma=False,
    )
```

profile of v0, /device:TPU:0, one launch (start us, length us, event | category | flops | bytes accessed | tf_op | source)
XLA Modules:
  0.0 96.2 jit_solution(4603364310684311930)
XLA Ops:
  0.0 0.0 copy-start.3
  0.0 2.7 %copy.66 = bf16[8,16,8,768]{3,2,0,1:T(8,128)(2,1)} copy(bf16[8,16,8,768]{3,2,1,0:T(8,128)(2,1)} %bitcast.149) | data formatting | bytes 3145728 | tf_op jit(solution)/shard_map/all_to_all | solution.py:78
  2.7 8.3 %all-to-all-start = ((bf16[64,16,768]{2,0,1:T(8,128)(2,1)}), bf16[64,16,768]{2,0,1:T(8,128)(2,1)S(1)}, u32[]{:S(2)}, u32[]{:S(2)}) async-start(bf16[64,16,768]{2,0,1:T(8,128)(2,1)} %bitcast.139), calls=%async_computation | async-start | bytes 3145728 | tf_op jit(solution)/shard_map/all_to_all | solution.py:78
  11.2 0.0 copy-done.3
  11.2 0.1 dynamic-slice_compare_fusion.2
  11.3 0.1 copy.24
  11.4 0.1 dynamic-slice_compare_fusion.1
  11.4 0.1 copy.33
  11.5 0.1 copy.35
  11.7 0.3 broadcast_in_dim.118
  12.0 0.9 bitcast_or_fusion
  13.0 1.1 %fusion.84 = (pred[1024,512]{0,1:T(8,128)(4,1)}, pred[1024,512]{0,1:T(8,128)(4,1)}) fusion(pred[1024,1024]{0,1:T(8,128)(4,1)S(1)} %bitcast_or_fusion), kind=kLoop, calls=%fused_computation.100 | loop fusion | bytes 2097152 | tf_op jit(solution)/shard_map/slice | solution.py:53
  14.0 0.2 broadcast_in_dim.126
  14.2 0.2 broadcast_in_dim.124
  14.4 1.0 bitcast_or_fusion.2
  15.4 29.8 %all-to-all-done = bf16[64,16,768]{2,0,1:T(8,128)(2,1)S(1)} async-done(((bf16[64,16,768]{2,0,1:T(8,128)(2,1)}), bf16[64,16,768]{2,0,1:T(8,128)(2,1)S(1)}, u32[]{:S(2)}, u32[]{:S(2)}) %all-to-all-start) | async-done | bytes 1572896 | tf_op jit(solution)/shard_map/all_to_all | solution.py:78
  45.2 0.0 copy-start
  45.2 1.2 %copy-done = bf16[64,16,768]{2,0,1:T(8,128)(2,1)} copy-done((bf16[64,16,768]{2,0,1:T(8,128)(2,1)}, bf16[64,16,768]{2,0,1:T(8,128)(2,1)S(1)}, u32[]{:S(2)}) %copy-start) | copy-done | bytes 1572888
  46.3 4.2 %reshape.241 = bf16[1024,2,3,128]{3,2,1,0:T(4,128)(2,1)S(1)} reshape(bf16[16,64,768]{2,1,0:T(8,128)(2,1)} %bitcast.144) | data formatting | bytes 3145728 | tf_op jit(solution)/shard_map/reshape | solution.py:81
  50.5 0.7 slice.56
  51.2 0.0 copy-start.2
  51.3 1.9 %fusion.83 = (bf16[512,2,1,128]{3,2,1,0:T(2,128)(2,1)S(1)}, bf16[512,2,1,128]{3,2,1,0:T(2,128)(2,1)S(1)}, bf16[512,2,1,128]{3,2,1,0:T(2,128)(2,1)S(1)}, bf16[512,2,1,128]{3,2,1,0:T(2,128)(2,1)S(1)}) fusion(bf16[1024,2,3,128]{3,2,1,0:T(4,128)(2,1)S(1)} %reshape.241), kind=kLoop, calls=%fused_computation.99 | loop fusion | bytes 2097152 | tf_op jit(solution)/shard_map/slice | solution.py:62
  53.3 0.0 copy-start.1
  53.4 0.1 collective-permute-start.3
  53.5 0.5 collective-permute-start
  54.0 0.1 collective-permute-start.2
  54.1 0.4 collective-permute-start.1
  54.5 0.0 copy-done.2
  54.5 1.0 %fusion = (f32[1024,2]{0,1:T(2,128)S(1)}, f32[2,512,1024]{2,1,0:T(8,128)S(1)}) fusion(pred[1024,512]{0,1:T(8,128)(4,1)S(1)} %copy-done.2, bf16[512,2,128]{2,0,1:T(8,128)(2,1)S(1)} %bitcast.155, bf16[1024,2,1,128]{3,2,1,0:T(2,128)(2,1)S(1)} %slice.56), kind=kOutput, calls=%fused_computation.9 | convolution fusion | flops 271579136 | bytes 5513216 | tf_op jit(solution)/shard_map/qhd,khd->qhk/dot_general | solution.py:45
  55.6 0.0 copy-done.1
  55.6 1.0 %fusion.1 = (f32[1024,2]{0,1:T(2,128)S(1)}, f32[2,512,1024]{2,1,0:T(8,128)S(1)}) fusion(pred[1024,512]{0,1:T(8,128)(4,1)S(1)} %copy-done.1, bf16[512,2,128]{2,0,1:T(8,128)(2,1)S(1)} %bitcast.157, bf16[1024,2,1,128]{3,2,1,0:T(2,128)(2,1)S(1)} %slice.56), kind=kOutput, calls=%fused_computation.10 | convolution fusion | flops 271579136 | bytes 5513216 | tf_op jit(solution)/shard_map/qhd,khd->qhk/dot_general | solution.py:45
  56.6 0.0 collective-permute-done.2
  56.6 1.0 %fusion.3 = (f32[1024,2]{0,1:T(2,128)S(1)}, f32[2,512,1024]{2,1,0:T(8,128)S(1)}) fusion(pred[1024,512]{0,1:T(8,128)(4,1)S(1)} %get-tuple-element.62, bf16[512,2,128]{2,0,1:T(8,128)(2,1)S(1)} %collective-permute-done.2, bf16[1024,2,1,128]{3,2,1,0:T(2,128)(2,1)S(1)} %slice.56), kind=kOutput, calls=%fused_computation.12 | convolution fusion | flops 271579136 | bytes 5513216 | tf_op jit(solution)/shard_map/while/body/eval_jaxpr/qhd,khd->qhk/dot_general | solution.py:45
  57.6 0.0 collective-permute-done
  57.6 1.0 %fusion.2 = (f32[1024,2]{0,1:T(2,128)S(1)}, f32[2,512,1024]{2,1,0:T(8,128)S(1)}) fusion(pred[1024,512]{0,1:T(8,128)(4,1)S(1)} %get-tuple-element.61, bf16[512,2,128]{2,0,1:T(8,128)(2,1)S(1)} %collective-permute-done, bf16[1024,2,1,128]{3,2,1,0:T(2,128)(2,1)S(1)} %slice.56), kind=kOutput, calls=%fused_computation.11 | convolution fusion | flops 271579136 | bytes 5513216 | tf_op jit(solution)/shard_map/while/body/eval_jaxpr/qhd,khd->qhk/dot_general | solution.py:45
  58.7 2.3 %fusion.4 = (f32[1024,2]{0,1:T(2,128)S(1)}, f32[1024,2]{0,1:T(2,128)S(1)}) fusion(f32[2,512,1024]{2,1,0:T(8,128)S(1)} %get-tuple-element.70, f32[1024,2]{0,1:T(2,128)S(1)} %get-tuple-element.58, pred[1024,512]{0,1:T(8,128)(4,1)S(1)} %copy-done.2, f32[1024,2]{0,1:T(2,128)S(1)} %get-tuple-element.35, f32[2,512,1024]{2,1,0:T(8,128)S(1)} %get-tuple-element.68, ...), kind=kLoop, calls=%fused_computation.13 | loop fusion | flops 10481664 | bytes 9469952 | tf_op jit(solution)/shard_map/reduce_sum | solution.py:58
  61.0 2.4 %fusion.8 = (f32[1024,2]{0,1:T(2,128)S(1)}, f32[1024,2]{0,1:T(2,128)S(1)}) fusion(f32[2,512,1024]{2,1,0:T(8,128)S(1)} %get-tuple-element.66, f32[1024,2]{0,1:T(2,128)S(1)} %get-tuple-element.34, pred[1024,512]{0,1:T(8,128)(4,1)S(1)} %get-tuple-element.61, f32[1024,2]{0,1:T(2,128)S(1)} %get-tuple-element.33, f32[2,512,1024]{2,1,0:T(8,128)S(1)} %get-tuple-element.64, ...), kind=kLoop, calls=%fused_computation.17 | loop fusion | flops 10481664 | bytes 9469952 | tf_op jit(solution)/shard_map/while/body/eval_jaxpr/reduce_sum | solution.py:58
  63.5 2.3 %fusion.45 = f32[1024,2,128]{2,0,1:T(8,128)S(1)} fusion(bf16[512,2,128]{2,0,1:T(8,128)(2,1)S(1)} %bitcast.151, f32[2,512,1024]{2,1,0:T(8,128)S(1)} %get-tuple-element.70, f32[1024,2]{0,1:T(2,128)S(1)} %get-tuple-element.58, pred[1024,512]{0,1:T(8,128)(4,1)S(1)} %copy-done.2, f32[1024,2]{0,1:T(2,128)S(1)} %get-tuple-element.32, ...), kind=kOutput, calls=%fused_computation.39 | convolution fusion | flops 274202624 | bytes 6053888 | tf_op jit(solution)/shard_map/qhk,khd->qhd/dot_general | solution.py:59
  65.8 2.0 %fusion.48 = f32[1024,2,128]{2,0,1:T(8,128)S(1)} fusion(f32[1024,2,128]{2,0,1:T(8,128)S(1)} %fusion.45, bf16[512,2,128]{2,0,1:T(8,128)(2,1)S(1)} %bitcast.153, f32[2,512,1024]{2,1,0:T(8,128)S(1)} %get-tuple-element.68, f32[1024,2]{0,1:T(2,128)S(1)} %get-tuple-element.35, pred[1024,512]{0,1:T(8,128)(4,1)S(1)} %copy-done.1, f32[1024,2]{0,1:T(2,128)S(1)} %get-tuple-element.31), kind=kOutput, calls=%fused_computation.40 | convolution fusion | flops 274202624 | bytes 7094272 | tf_op jit(solution)/shard_map/qhk,khd->qhd/dot_general | solution.py:59
  67.8 0.0 collective-permute-done.3
  67.8 1.7 %fusion.33 = f32[1024,2,128]{2,0,1:T(8,128)S(1)} fusion(bf16[512,2,128]{2,0,1:T(8,128)(2,1)S(1)} %collective-permute-done.3, f32[2,512,1024]{2,1,0:T(8,128)S(1)} %get-tuple-element.64, f32[1024,2]{0,1:T(2,128)S(1)} %get-tuple-element.33, pred[1024,512]{0,1:T(8,128)(4,1)S(1)} %get-tuple-element.62), kind=kOutput, calls=%fused_computation.35 | convolution fusion | flops 273678336 | bytes 6037504 | tf_op jit(solution)/shard_map/while/body/eval_jaxpr/qhk,khd->qhd/dot_general | solution.py:59
  69.5 0.0 collective-permute-done.1
  69.5 2.2 %divide_convert_fusion = bf16[1024,2,128]{2,0,1:T(8,128)(2,1)S(1)} fusion(f32[1024,2,128]{2,0,1:T(8,128)S(1)} %fusion.33, f32[1024,2,128]{2,0,1:T(8,128)S(1)} %fusion.48, bf16[512,2,128]{2,0,1:T(8,128)(2,1)S(1)} %collective-permute-done.1, f32[2,512,1024]{2,1,0:T(8,128)S(1)} %get-tuple-element.66, f32[1024,2]{0,1:T(2,128)S(1)} %get-tuple-element.34, ...), kind=kOutput, calls=%fused_computation.43 | convolution fusion | flops 274989056 | bytes 7626752 | tf_op jit(solution)/shard_map/while/body/eval_jaxpr/qhk,khd->qhd/dot_general | solution.py:59
  71.7 0.5 copy.37
  72.2 0.3 all_to_all.29
  72.5 22.9 %all_to_all.35 = bf16[16,64,256]{2,1,0:T(8,128)(2,1)S(1)} all-to-all(bf16[16,64,256]{2,1,0:T(8,128)(2,1)S(1)} %all_to_all.29), channel_id=1, replica_groups=mesh['blk'=2,'head'=16] {'head'}, dimensions={0} | all-to-all | bytes 1048576 | tf_op jit(solution)/shard_map/all_to_all | solution.py:127
  95.4 0.8 copy.49
  (9 shorter events, 0.3 us)
Async XLA Ops:
  0.0 11.2 %copy-start.3 = (s32[16,16]{1,0:T(8,128)S(1)}, s32[16,16]{1,0:T(8,128)}, u32[]{:S(2)}) copy-start(s32[16,16]{1,0:T(8,128)} %param.3) | copy-start | bytes 3076
  2.7 42.4 %all-to-all-start = ((bf16[64,16,768]{2,0,1:T(8,128)(2,1)}), bf16[64,16,768]{2,0,1:T(8,128)(2,1)S(1)}, u32[]{:S(2)}, u32[]{:S(2)}) async-start(bf16[64,16,768]{2,0,1:T(8,128)(2,1)} %bitcast.139), calls=%async_computation | async-start | bytes 3145728 | tf_op jit(solution)/shard_map/all_to_all | solution.py:78
  45.2 1.2 %copy-start = (bf16[64,16,768]{2,0,1:T(8,128)(2,1)}, bf16[64,16,768]{2,0,1:T(8,128)(2,1)S(1)}, u32[]{:S(2)}) copy-start(bf16[64,16,768]{2,0,1:T(8,128)(2,1)S(1)} %all-to-all-done) | copy-start | bytes 4718596
  51.2 3.3 %copy-start.2 = (pred[1024,512]{0,1:T(8,128)(4,1)S(1)}, pred[1024,512]{0,1:T(8,128)(4,1)}, u32[]{:S(2)}) copy-start(pred[1024,512]{0,1:T(8,128)(4,1)} %get-tuple-element.54) | copy-start | bytes 1572868
  53.3 2.3 %copy-start.1 = (pred[1024,512]{0,1:T(8,128)(4,1)S(1)}, pred[1024,512]{0,1:T(8,128)(4,1)}, u32[]{:S(2)}) copy-start(pred[1024,512]{0,1:T(8,128)(4,1)} %get-tuple-element.56) | copy-start | bytes 1572868
  53.4 14.4 %collective-permute-start.3 = (bf16[512,2,128]{2,0,1:T(8,128)(2,1)S(1)}, bf16[512,2,128]{2,0,1:T(8,128)(2,1)S(1)}, u32[]{:S(2)}, u32[]{:S(2)}) collective-permute-start(bf16[512,2,128]{2,0,1:T(8,128)(2,1)S(1)} %bitcast.152), channel_id=1, source_target_pairs={{0,16},{16,0},{1,17},{17,1},{2,18},{18,2},{3,19},{19,3},{4,20},{20... | collective-permute-start | bytes 786440 | tf_op jit(solution)/shard_map/while/body/eval_jaxpr/ppermute | solution.py:21
  53.5 4.1 %collective-permute-start = (bf16[512,2,128]{2,0,1:T(8,128)(2,1)S(1)}, bf16[512,2,128]{2,0,1:T(8,128)(2,1)S(1)}, u32[]{:S(2)}, u32[]{:S(2)}) collective-permute-start(bf16[512,2,128]{2,0,1:T(8,128)(2,1)S(1)} %bitcast.154), channel_id=1, source_target_pairs={{0,16},{16,0},{1,17},{17,1},{2,18},{18,2},{3,19},{19,3},{4,20},{20... | collective-permute-start | bytes 786440 | tf_op jit(solution)/shard_map/while/body/eval_jaxpr/ppermute | solution.py:21
  54.0 2.6 %collective-permute-start.2 = (bf16[512,2,128]{2,0,1:T(8,128)(2,1)S(1)}, bf16[512,2,128]{2,0,1:T(8,128)(2,1)S(1)}, u32[]{:S(2)}, u32[]{:S(2)}) collective-permute-start(bf16[512,2,128]{2,0,1:T(8,128)(2,1)S(1)} %bitcast.156), channel_id=1, source_target_pairs={{0,16},{16,0},{1,17},{17,1},{2,18},{18,2},{3,19},{19,3},{4,20},{20... | collective-permute-start | bytes 786440 | tf_op jit(solution)/shard_map/while/body/eval_jaxpr/ppermute | solution.py:21
  54.1 15.4 %collective-permute-start.1 = (bf16[512,2,128]{2,0,1:T(8,128)(2,1)S(1)}, bf16[512,2,128]{2,0,1:T(8,128)(2,1)S(1)}, u32[]{:S(2)}, u32[]{:S(2)}) collective-permute-start(bf16[512,2,128]{2,0,1:T(8,128)(2,1)S(1)} %bitcast.150), channel_id=1, source_target_pairs={{0,16},{16,0},{1,17},{17,1},{2,18},{18,2},{3,19},{19,3},{4,20},{20... | collective-permute-start | bytes 786440 | tf_op jit(solution)/shard_map/while/body/eval_jaxpr/ppermute | solution.py:21
where the time goes:
time: 96.5 us; the launch traced here: 96.2 us
  waiting for transfers between devices  29.8 us (31%)
  blocking collectives  22.9 us (24%)
  local copies, waits for them, and re-layouts  14.7 us (15%)
  matrix products  12.2 us (13%)
  starting transfers between devices  9.42 us (10%)
  other arithmetic  6.84 us (7%)
    all_to_all x1, waiting for transfers between devices, on_device(): lax.all_to_all(tokens_qkv, 'head', split_axis=1, concat_axis=0, tiled=True)  29.8 us
    all_to_all x1, blocking collectives, on_device(): lax.all_to_all(result, 'head', split_axis=0, concat_axis=1, tiled=True)  22.9 us
    all_to_all x1, starting transfers between devices, on_device(): lax.all_to_all(tokens_qkv, 'head', split_axis=1, concat_axis=0, tiled=True)  8.34 us
    dot_general x4, matrix products, attend(): jnp.einsum('qhk,khd->qhd', weights.astype(jnp.bfloat16), values_part[offs...  8.14 us
    reduce_sum x2, other arithmetic, attend(): totals = totals * factor + jnp.sum(weights, axis=-1)  4.69 us
    reshape x1, local copies, waits for them, and re-layouts, on_device(): packed = by_heads.reshape(rows_here, head_count, 3, HD)  4.16 us
    dot_general x4, matrix products, attend(): jnp.einsum('qhd,khd->qhk', queries, keys_part[offset:offset + stride], pr...  4.1 us
    all_to_all x1, local copies, waits for them, and re-layouts, on_device(): lax.all_to_all(tokens_qkv, 'head', split_axis=1, concat_axis=0, tiled=True)  2.74 us
  transfers between devices with their start and end apart: 5, of which 1 were waited for; matrix products, arithmetic and copies ran while one was open for 20% of the time, Pallas kernels for 0%

commit v1 on v0

--- a/solution.py
+++ b/solution.py
@@ -75,7 +75,12 @@
 
 
 def on_device(tokens_qkv, block_mask):
-    by_heads = lax.all_to_all(tokens_qkv, "head", split_axis=1, concat_axis=0, tiled=True)
+    by_heads = jnp.concatenate(
+        lax.all_to_all(
+            jnp.stack(jnp.split(tokens_qkv, lax.axis_size("head"), axis=1)), "head", 0, 0
+        ),
+        axis=0,
+    )
     rows_here = by_heads.shape[0]
     head_count = by_heads.shape[1] // (3 * HD)
     packed = by_heads.reshape(rows_here, head_count, 3, HD)

time: 96.5 us -> 124 us (1.28)
  local copies, waits for them, and re-layouts: 14.7 us -> 41.8 us
    unnamed x12 -> x27, local copies, waits for them, and re-layouts: 1.36 us -> 27.8 us
    another operation x0 -> x2, local copies, waits for them, and re-layouts: none -> 5.69 us  [the longest x1 4.16 us: on_device(): packed = by_heads.reshape(rows_here, head_count, 3, HD)]
    reshape x1 -> x0, local copies, waits for them, and re-layouts: 4.16 us -> none  [on_device(): packed = by_heads.reshape(rows_here, head_count, 3, HD)]
    all_to_all x1 -> x0, local copies, waits for them, and re-layouts: 2.74 us -> none  [on_device(): lax.all_to_all(tokens_qkv, 'head', split_axis=1, concat_axis=0, tiled=True)]
    dot_general x4, matrix products: 8.14 us -> 6.44 us  [attend(): jnp.einsum('qhk,khd->qhd', weights.astype(jnp.bfloat16), values_part[offs...]
    dot_general x4, matrix products: 4.1 us -> 5.44 us  [attend(): jnp.einsum('qhd,khd->qhk', queries, keys_part[offset:offset + stride], pr...]
  transfers between devices with their start and end apart: 5 -> 5, of which waited for: 1 -> 1; matrix products, arithmetic and copies ran while one was open for 20% -> 16% of each run, Pallas kernels for 0% -> 0%
where the time goes in v1:
time: 124 us; the launch traced here: 123 us
  local copies, waits for them, and re-layouts  41.8 us (34%)
  waiting for transfers between devices  29.9 us (24%)
  blocking collectives  22.9 us (18%)
  matrix products  11.9 us (10%)
  starting transfers between devices  9.46 us (8%)
  other arithmetic  6.82 us (6%)
    all_to_all x1, waiting for transfers between devices, on_device(): lax.all_to_all(jnp.stack(jnp.split(tokens_qkv, lax.axis_size('head'), axi...  29.9 us
    unnamed x27, local copies, waits for them, and re-layouts  27.8 us
    all_to_all x1, blocking collectives, on_device(): lax.all_to_all(result, 'head', split_axis=0, concat_axis=1, tiled=True)  22.9 us
    all_to_all x1, starting transfers between devices, on_device(): lax.all_to_all(jnp.stack(jnp.split(tokens_qkv, lax.axis_size('head'), axi...  8.39 us
    dot_general x4, matrix products, attend(): jnp.einsum('qhk,khd->qhd', weights.astype(jnp.bfloat16), values_part[offs...  6.44 us
    dot_general x4, matrix products, attend(): jnp.einsum('qhd,khd->qhk', queries, keys_part[offset:offset + stride], pr...  5.44 us
    reduce_sum x2, other arithmetic, attend(): totals = totals * factor + jnp.sum(weights, axis=-1)  4.7 us
    another operation x1, local copies, waits for them, and re-layouts, on_device(): packed = by_heads.reshape(rows_here, head_count, 3, HD)  4.16 us
  transfers between devices with their start and end apart: 5, of which 1 were waited for; matrix products, arithmetic and copies ran while one was open for 16% of the time, Pallas kernels for 0%

profile of v1, /device:TPU:0, one launch (start us, length us, event | category | flops | bytes accessed | tf_op | source)
XLA Modules:
  0.0 123.1 jit_solution(18393822409372000905)
XLA Ops:
  0.0 1.5 %bitcast_dynamic-update-slice_fusion.15 = bf16[16,64,768]{2,1,0:T(8,128)(2,1)} fusion(bf16[64,12288]{1,0:T(8,128)(2,1)} %param.2), kind=kLoop, calls=%fused_computation.61 | loop fusion | bytes 196608
  1.5 1.5 %bitcast_dynamic-update-slice_fusion.14 = bf16[16,64,768]{2,1,0:T(8,128)(2,1)} fusion(bf16[16,64,768]{2,1,0:T(8,128)(2,1)} %bitcast_dynamic-update-slice_fusion.15, bf16[64,12288]{1,0:T(8,128)(2,1)} %param.2), kind=kLoop, calls=%fused_computation.60 | loop fusion | bytes 196608
  3.1 1.5 %bitcast_dynamic-update-slice_fusion.13 = bf16[16,64,768]{2,1,0:T(8,128)(2,1)} fusion(bf16[16,64,768]{2,1,0:T(8,128)(2,1)} %bitcast_dynamic-update-slice_fusion.14, bf16[64,12288]{1,0:T(8,128)(2,1)} %param.2), kind=kLoop, calls=%fused_computation.59 | loop fusion | bytes 196608
  4.6 1.5 %bitcast_dynamic-update-slice_fusion.12 = bf16[16,64,768]{2,1,0:T(8,128)(2,1)} fusion(bf16[16,64,768]{2,1,0:T(8,128)(2,1)} %bitcast_dynamic-update-slice_fusion.13, bf16[64,12288]{1,0:T(8,128)(2,1)} %param.2), kind=kLoop, calls=%fused_computation.58 | loop fusion | bytes 196608
  6.1 1.5 %bitcast_dynamic-update-slice_fusion.11 = bf16[16,64,768]{2,1,0:T(8,128)(2,1)} fusion(bf16[16,64,768]{2,1,0:T(8,128)(2,1)} %bitcast_dynamic-update-slice_fusion.12, bf16[64,12288]{1,0:T(8,128)(2,1)} %param.2), kind=kLoop, calls=%fused_computation.57 | loop fusion | bytes 196608
  7.7 1.5 %bitcast_dynamic-update-slice_fusion.10 = bf16[16,64,768]{2,1,0:T(8,128)(2,1)} fusion(bf16[16,64,768]{2,1,0:T(8,128)(2,1)} %bitcast_dynamic-update-slice_fusion.11, bf16[64,12288]{1,0:T(8,128)(2,1)} %param.2), kind=kLoop, calls=%fused_computation.56 | loop fusion | bytes 196608
  9.2 1.5 %bitcast_dynamic-update-slice_fusion.9 = bf16[16,64,768]{2,1,0:T(8,128)(2,1)} fusion(bf16[16,64,768]{2,1,0:T(8,128)(2,1)} %bitcast_dynamic-update-slice_fusion.10, bf16[64,12288]{1,0:T(8,128)(2,1)} %param.2), kind=kLoop, calls=%fused_computation.55 | loop fusion | bytes 196608
  10.7 1.5 %bitcast_dynamic-update-slice_fusion.8 = bf16[16,64,768]{2,1,0:T(8,128)(2,1)} fusion(bf16[16,64,768]{2,1,0:T(8,128)(2,1)} %bitcast_dynamic-update-slice_fusion.9, bf16[64,12288]{1,0:T(8,128)(2,1)} %param.2), kind=kLoop, calls=%fused_computation.54 | loop fusion | bytes 196608
  12.3 1.5 %bitcast_dynamic-update-slice_fusion.7 = bf16[16,64,768]{2,1,0:T(8,128)(2,1)} fusion(bf16[16,64,768]{2,1,0:T(8,128)(2,1)} %bitcast_dynamic-update-slice_fusion.8, bf16[64,12288]{1,0:T(8,128)(2,1)} %param.2), kind=kLoop, calls=%fused_computation.53 | loop fusion | bytes 196608
  13.8 1.5 %bitcast_dynamic-update-slice_fusion.6 = bf16[16,64,768]{2,1,0:T(8,128)(2,1)} fusion(bf16[16,64,768]{2,1,0:T(8,128)(2,1)} %bitcast_dynamic-update-slice_fusion.7, bf16[64,12288]{1,0:T(8,128)(2,1)} %param.2), kind=kLoop, calls=%fused_computation.52 | loop fusion | bytes 196608
  15.3 1.5 %bitcast_dynamic-update-slice_fusion.5 = bf16[16,64,768]{2,1,0:T(8,128)(2,1)} fusion(bf16[16,64,768]{2,1,0:T(8,128)(2,1)} %bitcast_dynamic-update-slice_fusion.6, bf16[64,12288]{1,0:T(8,128)(2,1)} %param.2), kind=kLoop, calls=%fused_computation.51 | loop fusion | bytes 196608
  16.9 1.5 %bitcast_dynamic-update-slice_fusion.4 = bf16[16,64,768]{2,1,0:T(8,128)(2,1)} fusion(bf16[16,64,768]{2,1,0:T(8,128)(2,1)} %bitcast_dynamic-update-slice_fusion.5, bf16[64,12288]{1,0:T(8,128)(2,1)} %param.2), kind=kLoop, calls=%fused_computation.50 | loop fusion | bytes 196608
  18.4 1.5 %bitcast_dynamic-update-slice_fusion.3 = bf16[16,64,768]{2,1,0:T(8,128)(2,1)} fusion(bf16[16,64,768]{2,1,0:T(8,128)(2,1)} %bitcast_dynamic-update-slice_fusion.4, bf16[64,12288]{1,0:T(8,128)(2,1)} %param.2), kind=kLoop, calls=%fused_computation.49 | loop fusion | bytes 196608
  19.9 1.5 %bitcast_dynamic-update-slice_fusion.2 = bf16[16,64,768]{2,1,0:T(8,128)(2,1)} fusion(bf16[16,64,768]{2,1,0:T(8,128)(2,1)} %bitcast_dynamic-update-slice_fusion.3, bf16[64,12288]{1,0:T(8,128)(2,1)} %param.2), kind=kLoop, calls=%fused_computation.48 | loop fusion | bytes 196608
  21.4 1.5 %bitcast_dynamic-update-slice_fusion.1 = bf16[16,64,768]{2,1,0:T(8,128)(2,1)} fusion(bf16[16,64,768]{2,1,0:T(8,128)(2,1)} %bitcast_dynamic-update-slice_fusion.2, bf16[64,12288]{1,0:T(8,128)(2,1)} %param.2), kind=kLoop, calls=%fused_computation.47 | loop fusion | bytes 196608
  23.0 1.5 %bitcast_dynamic-update-slice_fusion = bf16[16,64,768]{2,1,0:T(8,128)(2,1)} fusion(bf16[16,64,768]{2,1,0:T(8,128)(2,1)} %bitcast_dynamic-update-slice_fusion.1, bf16[64,12288]{1,0:T(8,128)(2,1)} %param.2), kind=kLoop, calls=%fused_computation.46 | loop fusion | bytes 196608 | tf_op jit(solution)/shard_map/stack | solution.py:80
  24.5 8.4 %all-to-all-start = ((bf16[16,64,768]{2,1,0:T(8,128)(2,1)}), bf16[16,64,768]{2,1,0:T(8,128)(2,1)}, u32[]{:S(2)}, u32[]{:S(2)}) async-start(bf16[16,64,768]{2,1,0:T(8,128)(2,1)} %bitcast_dynamic-update-slice_fusion), calls=%async_computation | async-start | bytes 3145728 | tf_op jit(solution)/shard_map/all_to_all | solution.py:79
  33.3 0.1 copy.36
  33.5 0.3 broadcast_in_dim.118
  33.8 0.9 bitcast_or_fusion
  34.8 1.0 fusion.86
  35.8 0.2 broadcast_in_dim.126
  36.0 0.2 broadcast_in_dim.124
  36.2 0.9 bitcast_or_fusion.2
  37.2 29.9 %all-to-all-done = bf16[16,64,768]{2,1,0:T(8,128)(2,1)} async-done(((bf16[16,64,768]{2,1,0:T(8,128)(2,1)}), bf16[16,64,768]{2,1,0:T(8,128)(2,1)}, u32[]{:S(2)}, u32[]{:S(2)}) %all-to-all-start) | async-done | bytes 1572896 | tf_op jit(solution)/shard_map/all_to_all | solution.py:79
  67.1 4.2 %reshape_reshape.3 = bf16[1024,2,3,128]{3,2,1,0:T(4,128)(2,1)S(1)} reshape(bf16[16,64,768]{2,1,0:T(8,128)(2,1)} %all-to-all-done) | data formatting | bytes 3145728 | tf_op jit(solution)/shard_map/reshape;reshape | solution.py:86
  71.2 1.7 %slice.56 = bf16[1024,2,1,128]{3,2,1,0:T(2,128)(2,1)} slice(bf16[1024,2,3,128]{3,2,1,0:T(4,128)(2,1)S(1)} %reshape_reshape.3), slice={[0:1024], [0:2], [0:1], [0:128]} | slice | bytes 1048576 | tf_op jit(solution)/shard_map/slice | solution.py:87
  72.9 3.0 %fusion.85 = (bf16[512,2,1,128]{3,2,1,0:T(2,128)(2,1)}, bf16[512,2,1,128]{3,2,1,0:T(2,128)(2,1)}, bf16[512,2,1,128]{3,2,1,0:T(2,128)(2,1)}, bf16[512,2,1,128]{3,2,1,0:T(2,128)(2,1)}) fusion(bf16[1024,2,3,128]{3,2,1,0:T(4,128)(2,1)S(1)} %reshape_reshape.3), kind=kLoop, calls=%fused_computation.114 | loop fusion | bytes 2097152 | tf_op jit(solution)/shard_map/slice | solution.py:62
  75.9 1.2 %copy.48 = bf16[512,2,1,128]{0,3,1,2:T(8,128)(2,1)S(1)} copy(bf16[512,2,1,128]{3,2,1,0:T(2,128)(2,1)} %get-tuple-element.36) | data formatting | bytes 524288
  77.2 1.4 %copy.50 = bf16[512,2,1,128]{0,3,1,2:T(8,128)(2,1)S(1)} copy(bf16[512,2,1,128]{3,2,1,0:T(2,128)(2,1)} %get-tuple-element.38) | data formatting | bytes 524288
  78.6 1.1 copy.66
  79.6 1.1 copy.65
  80.8 0.5 collective-permute-start
  81.4 0.4 collective-permute-start.1
  81.8 2.4 %fusion.1 = (f32[1024,2]{0,1:T(2,128)S(1)}, f32[2,512,1024]{2,1,0:T(8,128)S(1)}) fusion(pred[1024,512]{0,1:T(8,128)(4,1)} %get-tuple-element.56, bf16[512,2,128]{2,0,1:T(8,128)(2,1)S(1)} %bitcast.176, bf16[1024,2,1,128]{3,2,1,0:T(2,128)(2,1)} %slice.56), kind=kOutput, calls=%fused_computation.10 | convolution fusion | flops 271579136 | bytes 5513216 | tf_op jit(solution)/shard_map/qhd,khd->qhk/dot_general | solution.py:45
  84.2 1.0 fusion
  85.3 1.0 fusion.2
  86.3 1.0 fusion.3
  87.4 2.3 %fusion.4 = (f32[1024,2]{0,1:T(2,128)S(1)}, f32[1024,2]{0,1:T(2,128)S(1)}) fusion(f32[2,512,1024]{2,1,0:T(8,128)S(1)} %get-tuple-element.70, f32[1024,2]{0,1:T(2,128)S(1)} %get-tuple-element.58, pred[1024,512]{0,1:T(8,128)(4,1)S(1)} %copy-done.1, f32[1024,2]{0,1:T(2,128)S(1)} %get-tuple-element.35, f32[2,512,1024]{2,1,0:T(8,128)S(1)} %get-tuple-element.68, ...), kind=kLoop, calls=%fused_computation.13 | loop fusion | flops 10481664 | bytes 9469952 | tf_op jit(solution)/shard_map/reduce_sum | solution.py:58
  89.6 2.4 %fusion.8 = (f32[1024,2]{0,1:T(2,128)S(1)}, f32[1024,2]{0,1:T(2,128)S(1)}) fusion(f32[2,512,1024]{2,1,0:T(8,128)S(1)} %get-tuple-element.66, f32[1024,2]{0,1:T(2,128)S(1)} %get-tuple-element.34, pred[1024,512]{0,1:T(8,128)(4,1)S(1)} %get-tuple-element.61, f32[1024,2]{0,1:T(2,128)S(1)} %get-tuple-element.33, f32[2,512,1024]{2,1,0:T(8,128)S(1)} %get-tuple-element.64, ...), kind=kLoop, calls=%fused_computation.17 | loop fusion | flops 10481664 | bytes 9469952 | tf_op jit(solution)/shard_map/while/body/eval_jaxpr/reduce_sum | solution.py:58
  92.1 1.7 %fusion.54 = f32[1024,2,128]{0,2,1:T(8,128)S(1)} fusion(f32[2,512,1024]{2,1,0:T(8,128)S(1)} %get-tuple-element.70, f32[1024,2]{0,1:T(2,128)S(1)} %get-tuple-element.58, pred[1024,512]{0,1:T(8,128)(4,1)S(1)} %copy-done.1, f32[1024,2]{0,1:T(2,128)S(1)} %get-tuple-element.32, f32[1024,2]{0,1:T(2,128)S(1)} %get-tuple-element.57, ...), kind=kOutput, calls=%fused_computation.41 | convolution fusion | flops 274202624 | bytes 6053888 | tf_op jit(solution)/shard_map/qhk,khd->qhd/dot_general | solution.py:59
  93.8 1.7 %fusion.48 = f32[1024,2,128]{0,2,1:T(8,128)S(1)} fusion(f32[1024,2,128]{0,2,1:T(8,128)S(1)} %fusion.54, f32[2,512,1024]{2,1,0:T(8,128)S(1)} %get-tuple-element.68, f32[1024,2]{0,1:T(2,128)S(1)} %get-tuple-element.35, pred[1024,512]{0,1:T(8,128)(4,1)S(1)} %copy-done, f32[1024,2]{0,1:T(2,128)S(1)} %get-tuple-element.31, bf16[512,2,1,128]{0,3,1,2:T(8,128)(2,1)S(1)} %copy.50), kind=kOutput, calls=%fused_computation.39 | convolution fusion | flops 274202624 | bytes 7094272 | tf_op jit(solution)/shard_map/qhk,khd->qhd/dot_general | solution.py:59
  95.5 1.5 %fusion.33 = f32[1024,2,128]{0,2,1:T(8,128)S(1)} fusion(bf16[512,2,128]{0,2,1:T(8,128)(2,1)S(1)} %collective-permute-done.3, f32[2,512,1024]{2,1,0:T(8,128)S(1)} %get-tuple-element.64, f32[1024,2]{0,1:T(2,128)S(1)} %get-tuple-element.33, pred[1024,512]{0,1:T(8,128)(4,1)S(1)} %get-tuple-element.62), kind=kOutput, calls=%fused_computation.34 | convolution fusion | flops 273678336 | bytes 6037504 | tf_op jit(solution)/shard_map/while/body/eval_jaxpr/qhk,khd->qhd/dot_general | solution.py:59
  97.0 1.6 %divide_convert_fusion = bf16[1024,2,128]{0,2,1:T(8,128)(2,1)S(1)} fusion(f32[1024,2,128]{0,2,1:T(8,128)S(1)} %fusion.33, f32[1024,2,128]{0,2,1:T(8,128)S(1)} %fusion.48, bf16[512,2,128]{0,2,1:T(8,128)(2,1)S(1)} %collective-permute-done.1, f32[2,512,1024]{2,1,0:T(8,128)S(1)} %get-tuple-element.66, f32[1024,2]{0,1:T(2,128)S(1)} %get-tuple-element.34, ...), kind=kOutput, calls=%fused_computation.42 | convolution fusion | flops 274989056 | bytes 7626752 | tf_op jit(solution)/shard_map/while/body/eval_jaxpr/qhk,khd->qhd/dot_general | solution.py:59
  98.6 0.4 copy.40
  99.0 0.3 all_to_all.18
  99.4 22.9 %all_to_all.24 = bf16[16,64,256]{2,1,0:T(8,128)(2,1)S(1)} all-to-all(bf16[16,64,256]{2,1,0:T(8,128)(2,1)S(1)} %all_to_all.18), channel_id=1, replica_groups=mesh['blk'=2,'head'=16] {'head'}, dimensions={0} | all-to-all | bytes 1048576 | tf_op jit(solution)/shard_map/all_to_all | solution.py:132
  122.2 0.8 copy.51
  (23 shorter events, 0.6 us)
Async XLA Ops:
  0.0 33.0 %copy-start.3 = (s32[16,16]{1,0:T(8,128)S(1)}, s32[16,16]{1,0:T(8,128)}, u32[]{:S(2)}) copy-start(s32[16,16]{1,0:T(8,128)} %param.3) | copy-start | bytes 3076
  24.5 42.6 %all-to-all-start = ((bf16[16,64,768]{2,1,0:T(8,128)(2,1)}), bf16[16,64,768]{2,1,0:T(8,128)(2,1)}, u32[]{:S(2)}, u32[]{:S(2)}) async-start(bf16[16,64,768]{2,1,0:T(8,128)(2,1)} %bitcast_dynamic-update-slice_fusion), calls=%async_computation | async-start | bytes 3145728 | tf_op jit(solution)/shard_map/all_to_all | solution.py:79
  77.2 7.1 %copy-start.1 = (pred[1024,512]{0,1:T(8,128)(4,1)S(1)}, pred[1024,512]{0,1:T(8,128)(4,1)}, u32[]{:S(2)}) copy-start(pred[1024,512]{0,1:T(8,128)(4,1)} %get-tuple-element.54) | copy-start | bytes 1572868
  77.2 7.1 %copy-start.2 = (bf16[1024,2,1,128]{3,2,1,0:T(2,128)(2,1)S(1)}, bf16[1024,2,1,128]{3,2,1,0:T(2,128)(2,1)}, u32[]{:S(2)}) copy-start(bf16[1024,2,1,128]{3,2,1,0:T(2,128)(2,1)} %slice.56) | copy-start | bytes 1572868
  80.7 5.6 %collective-permute-start.2 = (bf16[512,2,128]{2,0,1:T(8,128)(2,1)S(1)}, bf16[512,2,128]{2,0,1:T(8,128)(2,1)S(1)}, u32[]{:S(2)}, u32[]{:S(2)}) collective-permute-start(bf16[512,2,128]{2,0,1:T(8,128)(2,1)S(1)} %bitcast.175), channel_id=1, source_target_pairs={{0,16},{16,0},{1,17},{17,1},{2,18},{18,2},{3,19},{19,3},{4,20},{20... | collective-permute-start | bytes 786440 | tf_op jit(solution)/shard_map/while/body/eval_jaxpr/ppermute | solution.py:21
  80.8 4.5 %collective-permute-start = (bf16[512,2,128]{2,0,1:T(8,128)(2,1)S(1)}, bf16[512,2,128]{2,0,1:T(8,128)(2,1)S(1)}, u32[]{:S(2)}, u32[]{:S(2)}) collective-permute-start(bf16[512,2,128]{2,0,1:T(8,128)(2,1)S(1)} %bitcast.177), channel_id=1, source_target_pairs={{0,16},{16,0},{1,17},{17,1},{2,18},{18,2},{3,19},{19,3},{4,20},{20... | collective-permute-start | bytes 786440 | tf_op jit(solution)/shard_map/while/body/eval_jaxpr/ppermute | solution.py:21
  81.3 14.2 %collective-permute-start.3 = (bf16[512,2,128]{0,2,1:T(8,128)(2,1)S(1)}, bf16[512,2,128]{0,2,1:T(8,128)(2,1)S(1)}, u32[]{:S(2)}, u32[]{:S(2)}) collective-permute-start(bf16[512,2,128]{0,2,1:T(8,128)(2,1)S(1)} %bitcast.174), channel_id=1, source_target_pairs={{0,16},{16,0},{1,17},{17,1},{2,18},{18,2},{3,19},{19,3},{4,20},{20... | collective-permute-start | bytes 786440 | tf_op jit(solution)/shard_map/while/body/eval_jaxpr/ppermute | solution.py:21
  81.4 15.6 %collective-permute-start.1 = (bf16[512,2,128]{0,2,1:T(8,128)(2,1)S(1)}, bf16[512,2,128]{0,2,1:T(8,128)(2,1)S(1)}, u32[]{:S(2)}, u32[]{:S(2)}) collective-permute-start(bf16[512,2,128]{0,2,1:T(8,128)(2,1)S(1)} %bitcast.173), channel_id=1, source_target_pairs={{0,16},{16,0},{1,17},{17,1},{2,18},{18,2},{3,19},{19,3},{4,20},{20... | collective-permute-start | bytes 786440 | tf_op jit(solution)/shard_map/while/body/eval_jaxpr/ppermute | solution.py:21
  86.3 1.1 copy-start
